TPU v7x, 32 devices: a whole 2x2x4 slice. The times are simulated.
32 devices in a mesh: year: 4 (over z), row: 2 (over x), col: 4 (over y, core).
Axes of the slice: x: 2, y: 2, z: 4, core: 2. Of those that a mesh axis runs over, the one named last changes fastest.
Arguments:
- observed: float32 [4, 46, 128, 512], P('year', None, 'row', 'col'), may hold values from 0 to 0.8
- quality: int32 [4, 46, 128, 512], P('year', None, 'row', 'col'), may hold values from 0 to 3, as said below
- land_mask: int32 [128, 512], P('row', 'col'), may hold values 0 or 1
- params: float32 [4, 7, 128, 512], P('year', None, 'row', 'col'), may hold values from -0.3 to 3.4
- spatial_weight: float32 [7], replicated, may hold values from 0.2 to 2
- temporal_weight: float32 [7], replicated, may hold values from 0.2 to 2
Outputs:
- new_params: float32 [4, 7, 128, 512], P('year', None, 'row', 'col')
- residual: float32 [4, 7, 128, 512], P('year', None, 'row', 'col')
Inputs may be any that keep to these rules, and one draw needn't show every extreme that they name: `quality`: 0 good, 1 marginal, 2 snow, 3 cloud.
All inputs are finite; a program needn't handle non-finite values. No bound on the sum of `land_mask` on one device may be relied on, other than what follows from the above.
Results may differ from a plain program's by a relative error of at most 0.0003.
Values sent between devices are 32-bit elements; how exact they have to be, the bound alone decides.
A program may use at most 64 MiB of HBM per device.

v0:
```python
import jax
import jax.numpy as jnp
from jax import lax
from jax.sharding import PartitionSpec as P

ITERS = 4


damping = 0.1


def with_halo(cells, sides, width):
    for axis, dim in sides:
        count = lax.axis_size(axis)
        ends = count - 1
        head = lax.slice_in_dim(cells, 0, width, axis=dim)
        tail = lax.slice_in_dim(cells, cells.shape[dim] - width, cells.shape[dim], axis=dim)
        cells = jnp.concatenate(
            [
                lax.ppermute(tail, axis, [(i, (i + 1) % count) for i in range(ends)]),
                cells,
                lax.ppermute(head, axis, [((i + 1) % count, i) for i in range(ends)]),
            ],
            axis=dim,
        )
    return cells


def upper_pairs(count):
    return [
        (left_index, right_index)
        for left_index in range(count)
        for right_index in range(left_index, count)
    ]


def curve_terms(observed, quality, land_mask, params):
    num_dates = observed.shape[1]
    count = params.shape[1]
    weight = jnp.where(quality == 0, 1.0, 0.0) + jnp.where(quality == 1, 0.5, 0.0)
    weight = weight * land_mask.astype(jnp.float32)[None, None] / num_dates
    date_times = (jnp.arange(num_dates, dtype=jnp.float32) / num_dates).reshape(1, num_dates, 1, 1)
    level_base, peak_value, green_slope, rise_mid, rise_log, fall_mid, fall_log = [
        params[:, index][:, None] for index in range(count)
    ]
    rise_rate = jnp.exp(rise_log)
    fall_rate = jnp.exp(fall_log)
    rise_curve = jax.nn.sigmoid(rise_rate * (date_times - rise_mid))
    fall_curve = jax.nn.sigmoid(fall_rate * (date_times - fall_mid))
    season = rise_curve - fall_curve
    amplitude = peak_value - green_slope * date_times
    misfit = level_base + amplitude * season - observed
    rise_slope = rise_curve * (1.0 - rise_curve)
    fall_slope = fall_curve * (1.0 - fall_curve)
    jacobian = [
        jnp.ones_like(misfit),
        season,
        -date_times * season,
        -amplitude * rise_rate * rise_slope,
        amplitude * rise_slope * (date_times - rise_mid) * rise_rate,
        amplitude * fall_rate * fall_slope,
        -amplitude * fall_slope * (date_times - fall_mid) * fall_rate,
    ]
    weighted = [weight * column for column in jacobian]
    hessian = jnp.stack(
        [
            jnp.sum(weighted[left_index] * jacobian[right_index], axis=1)
            for left_index, right_index in upper_pairs(count)
        ]
    )
    gradient = jnp.stack(
        [jnp.sum(weighted[index] * misfit, axis=1) for index in range(count)], axis=1
    )
    return (hessian, gradient)


def blocks_from(hessian, count):
    blocks = [[None] * count for index in range(count)]
    for position, (left_index, right_index) in enumerate(upper_pairs(count)):
        blocks[left_index][right_index] = hessian[position]
        blocks[right_index][left_index] = hessian[position]
    return blocks


def block_apply(blocks, field):
    count = len(blocks)
    outputs = []
    for left_index in range(count):
        total = blocks[left_index][0] * field[:, 0]
        for right_index in range(1, count):
            total = total + blocks[left_index][right_index] * field[:, right_index]
        outputs.append(total)
    return jnp.stack(outputs, axis=1)


def invert(blocks):
    count = len(blocks)
    left_rows = [list(row) for row in blocks]
    right_rows = [
        [
            jnp.full_like(blocks[0][0], 1.0 if left_index == right_index else 0.0)
            for right_index in range(count)
        ]
        for left_index in range(count)
    ]
    for pivot in range(count):
        scale = 1.0 / left_rows[pivot][pivot]
        left_rows[pivot] = [entry * scale for entry in left_rows[pivot]]
        right_rows[pivot] = [entry * scale for entry in right_rows[pivot]]
        for other in range(count):
            if other != pivot:
                factor = left_rows[other][pivot]
                left_rows[other] = [
                    entry - factor * base_entry
                    for entry, base_entry in zip(left_rows[other], left_rows[pivot])
                ]
                right_rows[other] = [
                    entry - factor * base_entry
                    for entry, base_entry in zip(right_rows[other], right_rows[pivot])
                ]
    return right_rows


def prior_apply(field, spatial_weight, temporal_weight):
    num_years = field.shape[0]
    num_rows = field.shape[2]
    num_cols = field.shape[3]
    padded = with_halo(field, (("year", 0), ("row", 2), ("col", 3)), 1)
    year_pad = padded[:, :, 1:-1, 1:-1]
    plane_pad = padded[1:-1]
    year_pos = (
        lax.broadcasted_iota(jnp.int32, (num_years, 1, 1, 1), 0)
        + lax.axis_index("year") * num_years
    )
    row_pos = (
        lax.broadcasted_iota(jnp.int32, (1, 1, num_rows, 1), 2) + lax.axis_index("row") * num_rows
    )
    col_pos = (
        lax.broadcasted_iota(jnp.int32, (1, 1, 1, num_cols), 3) + lax.axis_index("col") * num_cols
    )
    year_low = jnp.where(year_pos == 0, field, year_pad[:-2])
    year_high = jnp.where(year_pos == num_years * lax.axis_size("year") - 1, field, year_pad[2:])
    row_low = jnp.where(row_pos == 0, field, plane_pad[:, :, :-2, 1:-1])
    row_high = jnp.where(
        row_pos == num_rows * lax.axis_size("row") - 1, field, plane_pad[:, :, 2:, 1:-1]
    )
    col_low = jnp.where(col_pos == 0, field, plane_pad[:, :, 1:-1, :-2])
    col_high = jnp.where(
        col_pos == num_cols * lax.axis_size("col") - 1, field, plane_pad[:, :, 1:-1, 2:]
    )
    plane = 4.0 * field - (row_low + row_high + col_low + col_high)
    yearly = 2.0 * field - (year_low + year_high)
    return (
        spatial_weight[None, :, None, None] * plane + temporal_weight[None, :, None, None] * yearly
    )


def paired_totals(residual, search, image):
    return lax.psum((jnp.sum(residual * search), jnp.sum(image * search)), ("year", "row", "col"))


def per_device(observed, quality, land_mask, params, spatial_weight, temporal_weight):
    count = params.shape[1]
    hessian, data_grad = curve_terms(observed, quality, land_mask, params)
    blocks = blocks_from(hessian, count)
    shifted = [list(row) for row in blocks]
    for index in range(count):
        shifted[index][index] = blocks[index][index] + (
            damping + 4.0 * spatial_weight[index] + 2.0 * temporal_weight[index]
        )
    precond = invert(shifted)

    def operate(field):
        return (
            block_apply(blocks, field)
            + damping * field
            + prior_apply(field, spatial_weight, temporal_weight)
        )

    residual = -(data_grad + prior_apply(params, spatial_weight, temporal_weight))
    step_field = jnp.zeros_like(params)
    search = block_apply(precond, residual)
    image = operate(search)
    inner_now, curvature = paired_totals(residual, search, image)
    step_len = inner_now / curvature
    direction, along = (search, image)
    for sweep in range(ITERS):
        step_field = step_field + step_len * direction
        residual = residual - step_len * along
        if sweep + 1 < ITERS:
            search = block_apply(precond, residual)
            image = operate(search)
            inner_next, curvature = paired_totals(residual, search, image)
            ratio = inner_next / inner_now
            step_len = inner_next / (curvature - ratio * inner_next / step_len)
            direction = search + ratio * direction
            along = image + ratio * along
            inner_now = inner_next
    return (params + step_field, residual)


def solution(mesh):
    return jax.shard_map(
        per_device,
        mesh=mesh,
        in_specs=(
            P("year", None, "row", "col"),
            P("year", None, "row", "col"),
            P("row", "col"),
            P("year", None, "row", "col"),
            P(),
            P(),
        ),
        out_specs=(P("year", None, "row", "col"), P("year", None, "row", "col")),
        check_vma=False,
    )
```

profile of v0, /device:TPU:0, one launch (start us, length us, event | category | flops | bytes accessed | tf_op | source)
XLA Modules:
  0.0 381.4 jit_solution(9251310727813972664)
XLA Ops:
  1.9 5.6 %collective-permute-start = (f32[1,7,64,128]{3,2,1,0:T(8,128)}, f32[1,7,64,128]{3,2,1,0:T(8,128)S(1)}, u32[]{:S(2)}, u32[]{:S(2)}) collective-permute-start(f32[1,7,64,128]{3,2,1,0:T(8,128)} %param.9), channel_id=1, source_target_pairs={{0,8},{8,16},{16,24},{1,9},{9,17},{17,25},{2,10},{10,18},{18,26},{... | collective-permute-start | bytes 688136 | tf_op jit(solution)/shard_map/ppermute | solution.py:20
  8.5 1.6 fusion.376
  14.5 1.6 fusion.375
  21.2 7.8 %multiply_reduce_fusion.21 = (f32[64,128]{1,0:T(8,128)S(1)}, f32[64,128]{1,0:T(8,128)S(1)}, f32[64,128]{1,0:T(8,128)S(1)}, f32[64,128]{1,0:T(8,128)S(1)}, f32[64...) fusion(f32[64,128]{1,0:T(8,128)S(1)} %get-tuple-element.256, ...), kind=kLoop, calls=%fused_computation.37 | loop fusion | flops 40411136 | bytes 4424048 | tf_op jit(solution)/shard_map/reduce_sum | solution.py:72
  40.0 4.5 %collective-permute-start.2 = (f32[3,7,1,128]{3,1,2,0:T(8,128)S(1)}, f32[3,7,1,128]{3,1,2,0:T(8,128)S(1)}, u32[]{:S(2)}, u32[]{:S(2)}) collective-permute-start(f32[3,7,1,128]{3,1,2,0:T(8,128)S(1)} %copy.122), channel_id=1, source_target_pairs={{0,4},{1,5},{2,6},{3,7},{8,12},{9,13},{10,14},{11,15},{16,20},{17,... | collective-permute-start | bytes 32264 | tf_op jit(solution)/shard_map/ppermute | solution.py:20
  44.6 1.3 collective-permute-done.2
  47.2 1.5 copy.78
  50.3 3.0 collective-permute-start.4
  56.2 1.6 fusion.67
  58.2 2.8 constant_dynamic-update-slice_fusion.23
  63.2 4.6 %collective-permute-start.6 = (f32[1,7,64,128]{3,2,1,0:T(8,128)S(1)}, f32[1,7,64,128]{3,2,1,0:T(8,128)S(1)}, u32[]{:S(2)}, u32[]{:S(2)}) collective-permute-start(f32[1,7,64,128]{3,2,1,0:T(8,128)S(1)} %constant_dynamic-update-slice_fusion.10), channel_id=1, source_target_pairs={{0,8},{8,16},{16,24},{1,9},{9,17},{17,25},{2,10},{10,18},{18,26},{... | collective-permute-start | bytes 688136 | tf_op jit(solution)/shard_map/ppermute | solution.py:20
  67.8 3.9 %collective-permute-done.7 = f32[1,7,64,128]{3,2,1,0:T(8,128)S(1)} collective-permute-done((f32[1,7,64,128]{3,2,1,0:T(8,128)S(1)}, f32[1,7,64,128]{3,2,1,0:T(8,128)S(1)}, u32[]{:S(2)}, u32[]{:S(2)}) %collective-permute-start.7) | collective-permute-done | bytes 229408 | tf_op jit(solution)/shard_map/ppermute | solution.py:22
  71.7 1.7 collective-permute-done.6
  74.8 4.5 %collective-permute-start.8 = (f32[3,7,1,128]{3,1,2,0:T(8,128)S(1)}, f32[3,7,1,128]{3,1,2,0:T(8,128)S(1)}, u32[]{:S(2)}, u32[]{:S(2)}) collective-permute-start(f32[3,7,1,128]{3,1,2,0:T(8,128)S(1)} %copy.124), channel_id=1, source_target_pairs={{0,4},{1,5},{2,6},{3,7},{8,12},{9,13},{10,14},{11,15},{16,20},{17,... | collective-permute-start | bytes 32264 | tf_op jit(solution)/shard_map/ppermute | solution.py:20
  79.4 1.3 collective-permute-done.8
  85.4 3.2 collective-permute-done.11
  89.0 2.2 multiply_reduce_fusion.34
  91.2 43.3 %all-reduce.3 = (f32[]{:T(128)}, f32[]{:T(128)}) all-reduce(f32[]{:T(128)} %get-tuple-element.46, f32[]{:T(128)} %get-tuple-element.45), channel_id=1, replica_groups=mesh['year'=4,'row'=2,'col'=4] {'year','row','col'}, use_global_device_ids=true, to_apply=%region_36.37 | all-reduce | flops 2 | bytes 16 | tf_op jit(solution)/shard_map/psum | solution.py:159
  135.9 1.6 constant_dynamic-update-slice_fusion.37
  137.8 1.5 collective-permute-start.13
  139.3 4.6 %collective-permute-start.12 = (f32[1,7,64,128]{3,2,1,0:T(8,128)S(1)}, f32[1,7,64,128]{3,2,1,0:T(8,128)S(1)}, u32[]{:S(2)}, u32[]{:S(2)}) collective-permute-start(f32[1,7,64,128]{3,2,1,0:T(8,128)S(1)} %constant_dynamic-update-slice_fusion.24), channel_id=1, source_target_pairs={{0,8},{8,16},{16,24},{1,9},{9,17},{17,25},{2,10},{10,18},{18,26},{... | collective-permute-start | bytes 688136 | tf_op jit(solution)/shard_map/ppermute | solution.py:20
  143.9 2.8 collective-permute-done.13
  149.2 4.5 %collective-permute-start.14 = (f32[3,7,1,128]{3,1,2,0:T(8,128)S(1)}, f32[3,7,1,128]{3,1,2,0:T(8,128)S(1)}, u32[]{:S(2)}, u32[]{:S(2)}) collective-permute-start(f32[3,7,1,128]{3,1,2,0:T(8,128)S(1)} %copy.126), channel_id=1, source_target_pairs={{0,4},{1,5},{2,6},{3,7},{8,12},{9,13},{10,14},{11,15},{16,20},{17,... | collective-permute-start | bytes 32264 | tf_op jit(solution)/shard_map/ppermute | solution.py:20
  153.8 1.3 collective-permute-done.14
  160.4 3.8 collective-permute-done.17
  165.3 2.9 multiply_reduce_fusion.32
  168.2 43.2 %all-reduce.2 = (f32[]{:T(128)}, f32[]{:T(128)}) all-reduce(f32[]{:T(128)} %get-tuple-element.44, f32[]{:T(128)} %get-tuple-element.43), channel_id=1, replica_groups=mesh['year'=4,'row'=2,'col'=4] {'year','row','col'}, use_global_device_ids=true, to_apply=%region_40.41 | all-reduce | flops 2 | bytes 16 | tf_op jit(solution)/shard_map/psum | solution.py:159
  216.8 1.6 constant_dynamic-update-slice_fusion.51
  220.1 4.6 %collective-permute-start.18 = (f32[1,7,64,128]{3,2,1,0:T(8,128)S(1)}, f32[1,7,64,128]{3,2,1,0:T(8,128)S(1)}, u32[]{:S(2)}, u32[]{:S(2)}) collective-permute-start(f32[1,7,64,128]{3,2,1,0:T(8,128)S(1)} %constant_dynamic-update-slice_fusion.38), channel_id=1, source_target_pairs={{0,8},{8,16},{16,24},{1,9},{9,17},{17,25},{2,10},{10,18},{18,26},{... | collective-permute-start | bytes 688136 | tf_op jit(solution)/shard_map/ppermute | solution.py:20
  224.7 2.7 collective-permute-done.19
  229.9 4.5 %collective-permute-start.20 = (f32[3,7,1,128]{3,1,2,0:T(8,128)S(1)}, f32[3,7,1,128]{3,1,2,0:T(8,128)S(1)}, u32[]{:S(2)}, u32[]{:S(2)}) collective-permute-start(f32[3,7,1,128]{3,1,2,0:T(8,128)S(1)} %copy.128), channel_id=1, source_target_pairs={{0,4},{1,5},{2,6},{3,7},{8,12},{9,13},{10,14},{11,15},{16,20},{17,... | collective-permute-start | bytes 32264 | tf_op jit(solution)/shard_map/ppermute | solution.py:20
  234.5 1.4 collective-permute-done.20
  237.7 2.1 copy.108
  239.8 1.9 collective-permute-start.22
  245.0 2.7 collective-permute-done.23
  247.7 2.0 copy.111
  249.7 2.8 multiply_reduce_fusion.30
  252.5 43.1 %all-reduce.1 = (f32[]{:T(128)}, f32[]{:T(128)}) all-reduce(f32[]{:T(128)} %get-tuple-element.42, f32[]{:T(128)} %get-tuple-element.41), channel_id=1, replica_groups=mesh['year'=4,'row'=2,'col'=4] {'year','row','col'}, use_global_device_ids=true, to_apply=%region_44.45 | all-reduce | flops 2 | bytes 16 | tf_op jit(solution)/shard_map/psum | solution.py:159
  300.6 1.6 constant_dynamic-update-slice_fusion.65
  303.9 4.6 %collective-permute-start.24 = (f32[1,7,64,128]{3,2,1,0:T(8,128)S(1)}, f32[1,7,64,128]{3,2,1,0:T(8,128)S(1)}, u32[]{:S(2)}, u32[]{:S(2)}) collective-permute-start(f32[1,7,64,128]{3,2,1,0:T(8,128)S(1)} %constant_dynamic-update-slice_fusion.52), channel_id=1, source_target_pairs={{0,8},{8,16},{16,24},{1,9},{9,17},{17,25},{2,10},{10,18},{18,26},{... | collective-permute-start | bytes 688136 | tf_op jit(solution)/shard_map/ppermute | solution.py:20
  308.4 2.8 collective-permute-done.25
  313.8 4.5 %collective-permute-start.26 = (f32[3,7,1,128]{3,1,2,0:T(8,128)S(1)}, f32[3,7,1,128]{3,1,2,0:T(8,128)S(1)}, u32[]{:S(2)}, u32[]{:S(2)}) collective-permute-start(f32[3,7,1,128]{3,1,2,0:T(8,128)S(1)} %copy.130), channel_id=1, source_target_pairs={{0,4},{1,5},{2,6},{3,7},{8,12},{9,13},{10,14},{11,15},{16,20},{17,... | collective-permute-start | bytes 32264 | tf_op jit(solution)/shard_map/ppermute | solution.py:20
  318.4 1.4 collective-permute-done.26
  321.0 1.5 copy.118
  322.4 1.3 collective-permute-start.28
  325.8 3.7 collective-permute-done.29
  330.7 2.0 multiply_reduce_fusion.28
  332.7 43.1 %all-reduce = (f32[]{:T(128)}, f32[]{:T(128)}) all-reduce(f32[]{:T(128)} %get-tuple-element.40, f32[]{:T(128)} %get-tuple-element.39), channel_id=1, replica_groups=mesh['year'=4,'row'=2,'col'=4] {'year','row','col'}, use_global_device_ids=true, to_apply=%region_48.49 | all-reduce | flops 2 | bytes 16 | tf_op jit(solution)/shard_map/psum | solution.py:159
  (328 shorter events, 58.1 us)
Async XLA Ops:
  0.6 38.0 %collective-permute-start.1 = (f32[1,7,64,128]{3,2,1,0:T(8,128)}, f32[1,7,64,128]{3,2,1,0:T(8,128)S(1)}, u32[]{:S(2)}, u32[]{:S(2)}) collective-permute-start(f32[1,7,64,128]{3,2,1,0:T(8,128)} %param.9), channel_id=1, source_target_pairs={{8,0},{16,8},{24,16},{9,1},{17,9},{25,17},{10,2},{18,10},{26,18},{... | collective-permute-start | bytes 688136 | tf_op jit(solution)/shard_map/ppermute | solution.py:22
  1.9 36.6 %collective-permute-start = (f32[1,7,64,128]{3,2,1,0:T(8,128)}, f32[1,7,64,128]{3,2,1,0:T(8,128)S(1)}, u32[]{:S(2)}, u32[]{:S(2)}) collective-permute-start(f32[1,7,64,128]{3,2,1,0:T(8,128)} %param.9), channel_id=1, source_target_pairs={{0,8},{8,16},{16,24},{1,9},{9,17},{17,25},{2,10},{10,18},{18,26},{... | collective-permute-start | bytes 688136 | tf_op jit(solution)/shard_map/ppermute | solution.py:20
  29.1 31.9 %copy-start.7 = (f32[64,128]{1,0:T(8,128)}, f32[64,128]{1,0:T(8,128)S(1)}, u32[]{:S(2)}) copy-start(f32[64,128]{1,0:T(8,128)S(1)} %get-tuple-element.28) | copy-start | bytes 98308
  29.1 32.0 %copy-start.4 = (f32[64,128]{1,0:T(8,128)}, f32[64,128]{1,0:T(8,128)S(1)}, u32[]{:S(2)}) copy-start(f32[64,128]{1,0:T(8,128)S(1)} %get-tuple-element.32) | copy-start | bytes 98308
  30.9 6.3 %copy-start.14 = (f32[1,1,64,128]{3,2,1,0:T(8,128)}, f32[1,1,64,128]{3,2,1,0:T(8,128)S(1)}, u32[]{:S(2)}) copy-start(f32[1,1,64,128]{3,2,1,0:T(8,128)S(1)} %get-tuple-element.185) | copy-start | bytes 98308
  30.9 6.3 %copy-start.16 = (f32[1,1,64,128]{3,2,1,0:T(8,128)}, f32[1,1,64,128]{3,2,1,0:T(8,128)S(1)}, u32[]{:S(2)}) copy-start(f32[1,1,64,128]{3,2,1,0:T(8,128)S(1)} %get-tuple-element.187) | copy-start | bytes 98308
  30.9 6.3 %copy-start.22 = (f32[1,1,64,128]{3,2,1,0:T(8,128)}, f32[1,1,64,128]{3,2,1,0:T(8,128)S(1)}, u32[]{:S(2)}) copy-start(f32[1,1,64,128]{3,2,1,0:T(8,128)S(1)} %get-tuple-element.183) | copy-start | bytes 98308
  38.7 5.9 %collective-permute-start.3 = (f32[3,7,1,128]{3,1,2,0:T(8,128)S(1)}, f32[3,7,1,128]{3,1,2,0:T(8,128)S(1)}, u32[]{:S(2)}, u32[]{:S(2)}) collective-permute-start(f32[3,7,1,128]{3,1,2,0:T(8,128)S(1)} %copy.123), channel_id=1, source_target_pairs={{4,0},{5,1},{6,2},{7,3},{12,8},{13,9},{14,10},{15,11},{20,16},{21,... | collective-permute-start | bytes 32264 | tf_op jit(solution)/shard_map/ppermute | solution.py:22
  40.0 5.9 %collective-permute-start.2 = (f32[3,7,1,128]{3,1,2,0:T(8,128)S(1)}, f32[3,7,1,128]{3,1,2,0:T(8,128)S(1)}, u32[]{:S(2)}, u32[]{:S(2)}) collective-permute-start(f32[3,7,1,128]{3,1,2,0:T(8,128)S(1)} %copy.122), channel_id=1, source_target_pairs={{0,4},{1,5},{2,6},{3,7},{8,12},{9,13},{10,14},{11,15},{16,20},{17,... | collective-permute-start | bytes 32264 | tf_op jit(solution)/shard_map/ppermute | solution.py:20
  44.6 11.3 %copy-start.75 = (pred[64]{0:T(512)(128)(4,1)}, pred[64]{0:T(512)(128)(4,1)S(1)}, u32[]{:S(2)}) copy-start(pred[64]{0:T(512)(128)(4,1)S(1)} %get-tuple-element.294) | copy-start | bytes 196
  44.6 11.3 %copy-start.77 = (pred[64]{0:T(512)(128)(4,1)}, pred[64]{0:T(512)(128)(4,1)S(1)}, u32[]{:S(2)}) copy-start(pred[64]{0:T(512)(128)(4,1)S(1)} %get-tuple-element.295) | copy-start | bytes 196
  49.0 5.6 %collective-permute-start.5 = (f32[3,7,66,1]{2,1,3,0:T(8,128)S(1)}, f32[3,7,66,1]{2,1,3,0:T(8,128)S(1)}, u32[]{:S(2)}, u32[]{:S(2)}) collective-permute-start(f32[3,7,66,1]{2,1,3,0:T(8,128)S(1)} %copy.80), channel_id=1, source_target_pairs={{1,0},{2,1},{3,2},{5,4},{6,5},{7,6},{9,8},{10,9},{11,10},{13,12},{... | collective-permute-start | bytes 16640 | tf_op jit(solution)/shard_map/ppermute | solution.py:22
  50.3 3.9 %collective-permute-start.4 = (f32[3,7,66,1]{2,1,3,0:T(8,128)S(1)}, f32[3,7,66,1]{2,1,3,0:T(8,128)S(1)}, u32[]{:S(2)}, u32[]{:S(2)}) collective-permute-start(f32[3,7,66,1]{2,1,3,0:T(8,128)S(1)} %copy.78), channel_id=1, source_target_pairs={{0,1},{1,2},{2,3},{4,5},{5,6},{6,7},{8,9},{9,10},{10,11},{12,13},{... | collective-permute-start | bytes 16640 | tf_op jit(solution)/shard_map/ppermute | solution.py:20
  61.9 9.8 %collective-permute-start.7 = (f32[1,7,64,128]{3,2,1,0:T(8,128)S(1)}, f32[1,7,64,128]{3,2,1,0:T(8,128)S(1)}, u32[]{:S(2)}, u32[]{:S(2)}) collective-permute-start(f32[1,7,64,128]{3,2,1,0:T(8,128)S(1)} %constant_dynamic-update-slice_fusion.10), channel_id=1, source_target_pairs={{8,0},{16,8},{24,16},{9,1},{17,9},{25,17},{10,2},{18,10},{26,18},{... | collective-permute-start | bytes 688136 | tf_op jit(solution)/shard_map/ppermute | solution.py:22
  63.2 10.2 %collective-permute-start.6 = (f32[1,7,64,128]{3,2,1,0:T(8,128)S(1)}, f32[1,7,64,128]{3,2,1,0:T(8,128)S(1)}, u32[]{:S(2)}, u32[]{:S(2)}) collective-permute-start(f32[1,7,64,128]{3,2,1,0:T(8,128)S(1)} %constant_dynamic-update-slice_fusion.10), channel_id=1, source_target_pairs={{0,8},{8,16},{16,24},{1,9},{9,17},{17,25},{2,10},{10,18},{18,26},{... | collective-permute-start | bytes 688136 | tf_op jit(solution)/shard_map/ppermute | solution.py:20
  73.4 8.3 %copy-start.2 = (f32[1,7,64,128]{3,2,1,0:T(8,128)}, f32[1,7,64,128]{3,2,1,0:T(8,128)S(1)}, u32[]{:S(2)}) copy-start(f32[1,7,64,128]{3,2,1,0:T(8,128)S(1)} %collective-permute-done.6) | copy-start | bytes 688132
  73.5 5.9 %collective-permute-start.9 = (f32[3,7,1,128]{3,1,2,0:T(8,128)S(1)}, f32[3,7,1,128]{3,1,2,0:T(8,128)S(1)}, u32[]{:S(2)}, u32[]{:S(2)}) collective-permute-start(f32[3,7,1,128]{3,1,2,0:T(8,128)S(1)} %copy.125), channel_id=1, source_target_pairs={{4,0},{5,1},{6,2},{7,3},{12,8},{13,9},{14,10},{15,11},{20,16},{21,... | collective-permute-start | bytes 32264 | tf_op jit(solution)/shard_map/ppermute | solution.py:22
  74.8 5.9 %collective-permute-start.8 = (f32[3,7,1,128]{3,1,2,0:T(8,128)S(1)}, f32[3,7,1,128]{3,1,2,0:T(8,128)S(1)}, u32[]{:S(2)}, u32[]{:S(2)}) collective-permute-start(f32[3,7,1,128]{3,1,2,0:T(8,128)S(1)} %copy.124), channel_id=1, source_target_pairs={{0,4},{1,5},{2,6},{3,7},{8,12},{9,13},{10,14},{11,15},{16,20},{17,... | collective-permute-start | bytes 32264 | tf_op jit(solution)/shard_map/ppermute | solution.py:20
  81.7 7.3 %copy-start.73 = (f32[7]{0:T(128)S(1)}, f32[7]{0:T(128)}, u32[]{:S(2)}) copy-start(f32[7]{0:T(128)} %param.10) | copy-start | bytes 88
  81.7 7.3 %copy-start.74 = (f32[7]{0:T(128)S(1)}, f32[7]{0:T(128)}, u32[]{:S(2)}) copy-start(f32[7]{0:T(128)} %param.11) | copy-start | bytes 88
  82.0 2.9 collective-permute-start.10
  83.7 4.9 %collective-permute-start.11 = (f32[3,7,66,1]{2,1,3,0:T(8,128)S(1)}, f32[3,7,66,1]{2,1,3,0:T(8,128)S(1)}, u32[]{:S(2)}, u32[]{:S(2)}) collective-permute-start(f32[3,7,66,1]{2,1,3,0:T(8,128)S(1)} %copy.90), channel_id=1, source_target_pairs={{1,0},{2,1},{3,2},{5,4},{6,5},{7,6},{9,8},{10,9},{11,10},{13,12},{... | collective-permute-start | bytes 16640 | tf_op jit(solution)/shard_map/ppermute | solution.py:22
  137.7 17.4 %copy-start.25 = (f32[1,7,64,128]{3,2,1,0:T(8,128)}, f32[1,7,64,128]{3,2,1,0:T(8,128)S(1)}, u32[]{:S(2)}) copy-start(f32[1,7,64,128]{3,2,1,0:T(8,128)S(1)} %get-tuple-element.275) | copy-start | bytes 688132
  137.8 8.8 %collective-permute-start.13 = (f32[1,7,64,128]{3,2,1,0:T(8,128)S(1)}, f32[1,7,64,128]{3,2,1,0:T(8,128)S(1)}, u32[]{:S(2)}, u32[]{:S(2)}) collective-permute-start(f32[1,7,64,128]{3,2,1,0:T(8,128)S(1)} %constant_dynamic-update-slice_fusion.24), channel_id=1, source_target_pairs={{8,0},{16,8},{24,16},{9,1},{17,9},{25,17},{10,2},{18,10},{26,18},{... | collective-permute-start | bytes 688136 | tf_op jit(solution)/shard_map/ppermute | solution.py:22
  139.3 8.5 %collective-permute-start.12 = (f32[1,7,64,128]{3,2,1,0:T(8,128)S(1)}, f32[1,7,64,128]{3,2,1,0:T(8,128)S(1)}, u32[]{:S(2)}, u32[]{:S(2)}) collective-permute-start(f32[1,7,64,128]{3,2,1,0:T(8,128)S(1)} %constant_dynamic-update-slice_fusion.24), channel_id=1, source_target_pairs={{0,8},{8,16},{16,24},{1,9},{9,17},{17,25},{2,10},{10,18},{18,26},{... | collective-permute-start | bytes 688136 | tf_op jit(solution)/shard_map/ppermute | solution.py:20
  146.7 8.5 %copy-start.1 = (f32[1,7,64,128]{3,2,1,0:T(8,128)}, f32[1,7,64,128]{3,2,1,0:T(8,128)S(1)}, u32[]{:S(2)}) copy-start(f32[1,7,64,128]{3,2,1,0:T(8,128)S(1)} %collective-permute-done.13) | copy-start | bytes 688132
  147.8 7.3 %copy-start.3 = (f32[1,7,64,128]{3,2,1,0:T(8,128)}, f32[1,7,64,128]{3,2,1,0:T(8,128)S(1)}, u32[]{:S(2)}) copy-start(f32[1,7,64,128]{3,2,1,0:T(8,128)S(1)} %collective-permute-done.12) | copy-start | bytes 688132
  147.9 5.9 %collective-permute-start.15 = (f32[3,7,1,128]{3,1,2,0:T(8,128)S(1)}, f32[3,7,1,128]{3,1,2,0:T(8,128)S(1)}, u32[]{:S(2)}, u32[]{:S(2)}) collective-permute-start(f32[3,7,1,128]{3,1,2,0:T(8,128)S(1)} %copy.127), channel_id=1, source_target_pairs={{4,0},{5,1},{6,2},{7,3},{12,8},{13,9},{14,10},{15,11},{20,16},{21,... | collective-permute-start | bytes 32264 | tf_op jit(solution)/shard_map/ppermute | solution.py:22
  149.2 5.9 %collective-permute-start.14 = (f32[3,7,1,128]{3,1,2,0:T(8,128)S(1)}, f32[3,7,1,128]{3,1,2,0:T(8,128)S(1)}, u32[]{:S(2)}, u32[]{:S(2)}) collective-permute-start(f32[3,7,1,128]{3,1,2,0:T(8,128)S(1)} %copy.126), channel_id=1, source_target_pairs={{0,4},{1,5},{2,6},{3,7},{8,12},{9,13},{10,14},{11,15},{16,20},{17,... | collective-permute-start | bytes 32264 | tf_op jit(solution)/shard_map/ppermute | solution.py:20
  157.1 2.9 collective-permute-start.16
  158.7 5.5 %collective-permute-start.17 = (f32[3,7,66,1]{2,1,3,0:T(8,128)S(1)}, f32[3,7,66,1]{2,1,3,0:T(8,128)}, u32[]{:S(2)}, u32[]{:S(2)}) collective-permute-start(f32[3,7,66,1]{2,1,3,0:T(8,128)S(1)} %copy.100), channel_id=1, source_target_pairs={{1,0},{2,1},{3,2},{5,4},{6,5},{7,6},{9,8},{10,9},{11,10},{13,12},{... | collective-permute-start | bytes 16640 | tf_op jit(solution)/shard_map/ppermute | solution.py:22
  218.7 17.2 %copy-start.26 = (f32[1,7,64,128]{3,2,1,0:T(8,128)}, f32[1,7,64,128]{3,2,1,0:T(8,128)S(1)}, u32[]{:S(2)}) copy-start(f32[1,7,64,128]{3,2,1,0:T(8,128)S(1)} %get-tuple-element.273) | copy-start | bytes 688132
  218.8 8.6 %collective-permute-start.19 = (f32[1,7,64,128]{3,2,1,0:T(8,128)S(1)}, f32[1,7,64,128]{3,2,1,0:T(8,128)S(1)}, u32[]{:S(2)}, u32[]{:S(2)}) collective-permute-start(f32[1,7,64,128]{3,2,1,0:T(8,128)S(1)} %constant_dynamic-update-slice_fusion.38), channel_id=1, source_target_pairs={{8,0},{16,8},{24,16},{9,1},{17,9},{25,17},{10,2},{18,10},{26,18},{... | collective-permute-start | bytes 688136 | tf_op jit(solution)/shard_map/ppermute | solution.py:22
  220.1 8.5 %collective-permute-start.18 = (f32[1,7,64,128]{3,2,1,0:T(8,128)S(1)}, f32[1,7,64,128]{3,2,1,0:T(8,128)S(1)}, u32[]{:S(2)}, u32[]{:S(2)}) collective-permute-start(f32[1,7,64,128]{3,2,1,0:T(8,128)S(1)} %constant_dynamic-update-slice_fusion.38), channel_id=1, source_target_pairs={{0,8},{8,16},{16,24},{1,9},{9,17},{17,25},{2,10},{10,18},{18,26},{... | collective-permute-start | bytes 688136 | tf_op jit(solution)/shard_map/ppermute | solution.py:20
  228.6 5.9 %collective-permute-start.21 = (f32[3,7,1,128]{3,1,2,0:T(8,128)S(1)}, f32[3,7,1,128]{3,1,2,0:T(8,128)S(1)}, u32[]{:S(2)}, u32[]{:S(2)}) collective-permute-start(f32[3,7,1,128]{3,1,2,0:T(8,128)S(1)} %copy.129), channel_id=1, source_target_pairs={{4,0},{5,1},{6,2},{7,3},{12,8},{13,9},{14,10},{15,11},{20,16},{21,... | collective-permute-start | bytes 32264 | tf_op jit(solution)/shard_map/ppermute | solution.py:22
  229.9 5.9 %collective-permute-start.20 = (f32[3,7,1,128]{3,1,2,0:T(8,128)S(1)}, f32[3,7,1,128]{3,1,2,0:T(8,128)S(1)}, u32[]{:S(2)}, u32[]{:S(2)}) collective-permute-start(f32[3,7,1,128]{3,1,2,0:T(8,128)S(1)} %copy.128), channel_id=1, source_target_pairs={{0,4},{1,5},{2,6},{3,7},{8,12},{9,13},{10,14},{11,15},{16,20},{17,... | collective-permute-start | bytes 32264 | tf_op jit(solution)/shard_map/ppermute | solution.py:20
  237.7 11.9 %copy-start.76 = (pred[64]{0:T(512)(128)(4,1)S(1)}, pred[64]{0:T(512)(128)(4,1)}, u32[]{:S(2)}) copy-start(pred[64]{0:T(512)(128)(4,1)} %copy-done.75) | copy-start | bytes 196
  237.7 11.9 %copy-start.78 = (pred[64]{0:T(512)(128)(4,1)S(1)}, pred[64]{0:T(512)(128)(4,1)}, u32[]{:S(2)}) copy-start(pred[64]{0:T(512)(128)(4,1)} %copy-done.77) | copy-start | bytes 196
  239.8 4.1 %collective-permute-start.22 = (f32[3,7,66,1]{2,1,3,0:T(8,128)}, f32[3,7,66,1]{2,1,3,0:T(8,128)}, u32[]{:S(2)}, u32[]{:S(2)}) collective-permute-start(f32[3,7,66,1]{2,1,3,0:T(8,128)} %copy.108), channel_id=1, source_target_pairs={{0,1},{1,2},{2,3},{4,5},{5,6},{6,7},{8,9},{9,10},{10,11},{12,13},{... | collective-permute-start | bytes 16640 | tf_op jit(solution)/shard_map/ppermute | solution.py:20
  242.6 5.1 %collective-permute-start.23 = (f32[3,7,66,1]{2,1,3,0:T(8,128)}, f32[3,7,66,1]{2,1,3,0:T(8,128)}, u32[]{:S(2)}, u32[]{:S(2)}) collective-permute-start(f32[3,7,66,1]{2,1,3,0:T(8,128)} %copy.110), channel_id=1, source_target_pairs={{1,0},{2,1},{3,2},{5,4},{6,5},{7,6},{9,8},{10,9},{11,10},{13,12},{... | collective-permute-start | bytes 16640 | tf_op jit(solution)/shard_map/ppermute | solution.py:22
  302.6 8.7 %collective-permute-start.25 = (f32[1,7,64,128]{3,2,1,0:T(8,128)S(1)}, f32[1,7,64,128]{3,2,1,0:T(8,128)S(1)}, u32[]{:S(2)}, u32[]{:S(2)}) collective-permute-start(f32[1,7,64,128]{3,2,1,0:T(8,128)S(1)} %constant_dynamic-update-slice_fusion.52), channel_id=1, source_target_pairs={{8,0},{16,8},{24,16},{9,1},{17,9},{25,17},{10,2},{18,10},{26,18},{... | collective-permute-start | bytes 688136 | tf_op jit(solution)/shard_map/ppermute | solution.py:22
  303.9 8.6 %collective-permute-start.24 = (f32[1,7,64,128]{3,2,1,0:T(8,128)S(1)}, f32[1,7,64,128]{3,2,1,0:T(8,128)S(1)}, u32[]{:S(2)}, u32[]{:S(2)}) collective-permute-start(f32[1,7,64,128]{3,2,1,0:T(8,128)S(1)} %constant_dynamic-update-slice_fusion.52), channel_id=1, source_target_pairs={{0,8},{8,16},{16,24},{1,9},{9,17},{17,25},{2,10},{10,18},{18,26},{... | collective-permute-start | bytes 688136 | tf_op jit(solution)/shard_map/ppermute | solution.py:20
  312.5 5.9 %collective-permute-start.27 = (f32[3,7,1,128]{3,1,2,0:T(8,128)S(1)}, f32[3,7,1,128]{3,1,2,0:T(8,128)S(1)}, u32[]{:S(2)}, u32[]{:S(2)}) collective-permute-start(f32[3,7,1,128]{3,1,2,0:T(8,128)S(1)} %copy.131), channel_id=1, source_target_pairs={{4,0},{5,1},{6,2},{7,3},{12,8},{13,9},{14,10},{15,11},{20,16},{21,... | collective-permute-start | bytes 32264 | tf_op jit(solution)/shard_map/ppermute | solution.py:22
  313.8 5.9 %collective-permute-start.26 = (f32[3,7,1,128]{3,1,2,0:T(8,128)S(1)}, f32[3,7,1,128]{3,1,2,0:T(8,128)S(1)}, u32[]{:S(2)}, u32[]{:S(2)}) collective-permute-start(f32[3,7,1,128]{3,1,2,0:T(8,128)S(1)} %copy.130), channel_id=1, source_target_pairs={{0,4},{1,5},{2,6},{3,7},{8,12},{9,13},{10,14},{11,15},{16,20},{17,... | collective-permute-start | bytes 32264 | tf_op jit(solution)/shard_map/ppermute | solution.py:20
  321.0 9.7 %copy-start.80 = (pred[128]{0:T(512)(128)(4,1)S(1)}, pred[128]{0:T(512)(128)(4,1)}, u32[]{:S(2)}) copy-start(pred[128]{0:T(512)(128)(4,1)} %copy-done.79) | copy-start | bytes 388
  321.0 9.7 %copy-start.82 = (pred[128]{0:T(512)(128)(4,1)S(1)}, pred[128]{0:T(512)(128)(4,1)}, u32[]{:S(2)}) copy-start(pred[128]{0:T(512)(128)(4,1)} %copy-done.81) | copy-start | bytes 388
  322.4 3.0 collective-permute-start.28
  324.1 5.4 %collective-permute-start.29 = (f32[3,7,66,1]{2,1,3,0:T(8,128)S(1)}, f32[3,7,66,1]{2,1,3,0:T(8,128)S(1)}, u32[]{:S(2)}, u32[]{:S(2)}) collective-permute-start(f32[3,7,66,1]{2,1,3,0:T(8,128)S(1)} %copy.120), channel_id=1, source_target_pairs={{1,0},{2,1},{3,2},{5,4},{6,5},{7,6},{9,8},{10,9},{11,10},{13,12},{... | collective-permute-start | bytes 16640 | tf_op jit(solution)/shard_map/ppermute | solution.py:22
  (65 other events, 146.5 us)
where the time goes:
time: 384 us; the launch traced here: 381 us
  blocking collectives  173 us (45%)
  starting transfers between devices  74.9 us (20%)
  other arithmetic  40.5 us (11%)
  waiting for transfers between devices  38.4 us (10%)
  local copies, waits for them, and re-layouts  29.6 us (8%)
  between operations  25.2 us (7%)
    psum x4, blocking collectives, paired_totals(): lax.psum((jnp.sum(residual * search), jnp.sum(image * search)), ('year',...  173 us
    ppermute x15, starting transfers between devices, with_halo(): lax.ppermute(tail, axis, [(i, (i + 1) % count) for i in range(ends)])  55.3 us
    ppermute x15, waiting for transfers between devices, with_halo(): lax.ppermute(head, axis, [((i + 1) % count, i) for i in range(ends)])  25.7 us
    ppermute x15, starting transfers between devices, with_halo(): lax.ppermute(head, axis, [((i + 1) % count, i) for i in range(ends)])  19.6 us
    ppermute x15, waiting for transfers between devices, with_halo(): lax.ppermute(tail, axis, [(i, (i + 1) % count) for i in range(ends)])  12.8 us
    slice x11, local copies, waits for them, and re-layouts, with_halo(): lax.slice_in_dim(cells, cells.shape[dim] - width, cells.shape[dim], axis=...  10.3 us
    reduce_sum x4, other arithmetic, paired_totals(): jnp.sum(image * search)  9.9 us
    unnamed x24, other arithmetic  8.22 us
  transfers between devices with their start and end apart: 30, of which 18 were waited for; matrix products, arithmetic and copies ran while one was open for 7% of the time, Pallas kernels for 0%

commit v1 on v0

v1 whole, which is shorter than its diff:
```python
import functools

import jax
import jax.numpy as jnp
from jax import lax
from jax.experimental import pallas as pl
from jax.experimental.pallas import tpu as pltpu
from jax.sharding import PartitionSpec as P

ITERS = 4
ROUNDS = ITERS + 1
SUB = 8
BLOCKS = 2
DAMPING = 0.1
MESH = pl.DeviceIdType.MESH


def pairs_of(count):
    return [(i, j) for i in range(count) for j in range(i, count)]


def kernel(
    sizes,
    observed,
    quality,
    land,
    params,
    spatial,
    temporal,
    new_params,
    residual,
    obs,
    qual,
    field,
    inverse,
    resid,
    moments,
    plane_slots,
    year_slots,
    load_sem,
    send_sem,
    recv_sem,
    row_send,
    row_recv,
    plane_send,
    plane_recv,
    line_send,
    line_recv,
):
    n_year, n_row, n_col = sizes
    dates, rows, cols = obs.shape
    count = resid.shape[1]
    step_rows = SUB * BLOCKS
    chunks = rows // step_rows
    pairs = pairs_of(count)
    place = {pair: at for at, pair in enumerate(pairs)}

    year, row, col = lax.axis_index("year"), lax.axis_index("row"), lax.axis_index("col")
    even = lax.rem(row, 2) == 0

    has_prev, has_next = year > 0, year < n_year - 1
    has_left, has_right = col > 0, col < n_col - 1
    has_up, has_down = row > 0, row < n_row - 1
    has_first = jnp.logical_or(jnp.logical_and(even, has_up), jnp.logical_and(~even, has_down))
    has_last = jnp.logical_or(jnp.logical_and(even, has_down), jnp.logical_and(~even, has_up))
    toward_first = row + jnp.where(even, -1, 1)
    toward_last = row + jnp.where(even, 1, -1)

    def chunk_rows(position):
        chunk = jnp.where(even, position, chunks - 1 - position)
        return pl.multiple_of(chunk * step_rows, step_rows)

    param_load = pltpu.make_async_copy(
        params.at[0], field.at[0, 0, :, pl.ds(SUB, rows), :], load_sem.at[0]
    )
    param_load.start()

    def input_loads(position):
        start = chunk_rows(position)
        where = (slice(None), pl.ds(start, step_rows), slice(None))
        return (
            pltpu.make_async_copy(observed.at[0].at[where], obs.at[where], load_sem.at[1 + 2 * position]),
            pltpu.make_async_copy(quality.at[0].at[where], qual.at[where], load_sem.at[2 + 2 * position]),
        )

    for position in range(chunks):
        for copy in input_loads(position):
            copy.start()

    barrier = pltpu.get_barrier_semaphore()
    for other in range(1, n_row * n_col):
        spot = lax.rem(row * n_col + col + other, n_row * n_col)
        pl.semaphore_signal(
            barrier, inc=1, device_id=(year, spot // n_col, lax.rem(spot, n_col)), device_id_type=MESH
        )
    for other in range(1, n_year):
        pl.semaphore_signal(
            barrier, inc=1, device_id=(lax.rem(year + other, n_year), row, col), device_id_type=MESH
        )
    pl.semaphore_wait(barrier, n_row * n_col + n_year - 2)

    sides = (
        (has_next, (year + 1, row, col), 1, has_prev),
        (has_prev, (year - 1, row, col), 2, has_next),
        (has_right, (year, row, col + 1), 3, has_left),
        (has_left, (year, row, col - 1), 4, has_right),
    )

    def side_copy(step, position, side):
        _, target, slot, _ = sides[side]
        where = pl.ds(chunk_rows(position) + SUB, step_rows)
        return pltpu.make_async_remote_copy(
            src_ref=field.at[step, 0, :, where, :],
            dst_ref=field.at[step, slot, :, where, :],
            send_sem=send_sem.at[step, side, position],
            recv_sem=recv_sem.at[step, side, position],
            device_id=target,
            device_id_type=MESH,
        )

    def row_copy(step, last):
        top = jnp.logical_xor(even, last)
        source = pl.multiple_of(jnp.where(top, SUB, rows), SUB)
        target = pl.multiple_of(jnp.where(top, rows + SUB, 0), SUB)
        return pltpu.make_async_remote_copy(
            src_ref=field.at[step, 0, :, pl.ds(source, SUB), :],
            dst_ref=field.at[step, 0, :, pl.ds(target, SUB), :],
            send_sem=row_send.at[step, int(last)],
            recv_sem=row_recv.at[step, int(last)],
            device_id=(year, toward_last if last else toward_first, col),
            device_id_type=MESH,
        )

    def start_sends(step, position):
        for side in range(4):
            @pl.when(sides[side][0])
            def _(side=side):
                side_copy(step, position, side).start()

    def wait_sides(step, position):
        for side in range(4):
            @pl.when(sides[side][3])
            def _(side=side):
                side_copy(step, position, side).wait_recv()

    def close_edges(step, first, last):
        for flag, at_last, present in ((first, False, has_first), (last, True, has_last)):
            top = jnp.logical_xor(even, at_last)

            @pl.when(jnp.logical_and(flag, present))
            def _(at_last=at_last):
                row_copy(step, at_last).start()

            def repeat(source, edge, target):
                for p in range(count):
                    block = field[step, 0, p, source : source + SUB, :]
                    field[step, 0, p, target : target + SUB, :] = jnp.broadcast_to(
                        block[edge : edge + 1, :], (SUB, cols)
                    )

            @pl.when(jnp.logical_and(jnp.logical_and(flag, ~present), top))
            def _():
                repeat(SUB, 0, 0)

            @pl.when(jnp.logical_and(jnp.logical_and(flag, ~present), ~top))
            def _():
                repeat(rows, SUB - 1, rows + SUB)

    def wait_edges(step, first, last):
        for flag, at_last, present in ((first, False, has_first), (last, True, has_last)):
            @pl.when(jnp.logical_and(flag, present))
            def _(at_last=at_last):
                row_copy(step, at_last).wait_recv()

    param_load.wait()

    def send_params(position, carry):
        start_sends(0, position)
        return carry

    lax.fori_loop(0, chunks, send_params, 0)
    close_edges(0, True, True)

    prev_slot = jnp.where(has_prev, 1, 0)
    next_slot = jnp.where(has_next, 2, 0)
    left_slot = jnp.where(has_left, 3, 0)
    right_slot = jnp.where(has_right, 4, 0)
    lane = lax.broadcasted_iota(jnp.int32, (SUB, cols), 1)
    level = lax.broadcasted_iota(jnp.int32, (SUB, cols), 0)
    lane_first, lane_last = lane == 0, lane == cols - 1
    level_first, level_last = level == 0, level == SUB - 1
    grid_left = lane == jnp.where(has_left, -1, 0)
    grid_right = lane == jnp.where(has_right, -1, cols - 1)

    def around(step, p, start):
        own = pl.ds(start + SUB, SUB)
        here = field[step, 0, p, own, :]
        above = field[step, 0, p, pl.ds(start, SUB), :]
        below = field[step, 0, p, pl.ds(start + 2 * SUB, SUB), :]
        up = pltpu.roll(jnp.where(level_last, above, here), 1, 0)
        down = pltpu.roll(jnp.where(level_first, below, here), SUB - 1, 0)
        left = pltpu.roll(jnp.where(lane_last, field[step, left_slot, p, own, :], here), 1, 1)
        right = pltpu.roll(
            jnp.where(lane_first, field[step, right_slot, p, own, :], here), cols - 1, 1
        )
        left = jnp.where(grid_left, here, left)
        right = jnp.where(grid_right, here, right)
        plane = (up + down) + (left + right)
        yearly = field[step, prev_slot, p, own, :] + field[step, next_slot, p, own, :]
        return here, spatial[p] * plane + temporal[p] * yearly

    def precondition(start, values):
        rows_here = pl.ds(start, SUB)
        entry = [inverse[at, rows_here, :] for at in range(len(pairs))]
        outs = []
        for p in range(count):
            total = entry[place[(0, p)]] * values[0]
            for q in range(1, count):
                total = total + entry[place[(min(p, q), max(p, q))]] * values[q]
            outs.append(total)
        return outs

    def dot(left, right):
        terms = [a * b for a, b in zip(left, right)]
        while len(terms) > 1:
            terms = [sum(terms[i : i + 2][1:], terms[i]) for i in range(0, len(terms), 2)]
        return terms[0]

    def normal(start):
        here = pl.ds(start, SUB)
        base, peak, slope, rise_mid, rise_log, fall_mid, fall_log = [
            field[0, 0, p, pl.ds(start + SUB, SUB), :] for p in range(count)
        ]
        rise_rate, fall_rate = jnp.exp(rise_log), jnp.exp(fall_log)
        rise_half, fall_half = 0.5 * rise_rate, 0.5 * fall_rate

        def date_step(date, sums):
            time = date.astype(jnp.float32) * (1.0 / dates)
            flag = qual[date, here, :].astype(jnp.float32)
            weight = jnp.maximum(1.0 - 0.5 * flag, 0.0)
            rise_gap = time - rise_mid
            fall_gap = time - fall_mid
            rise = jnp.tanh(rise_half * rise_gap)
            fall = jnp.tanh(fall_half * fall_gap)
            season = rise - fall
            height = peak - slope * time
            rise_bell = height - height * (rise * rise)
            fall_bell = height - height * (fall * fall)
            basis = [
                None,
                season,
                time * season,
                rise_bell,
                rise_gap * rise_bell,
                fall_bell,
                fall_gap * fall_bell,
            ]
            weighted = [weight] + [weight * item for item in basis[1:]]
            out = []
            for i, j in pairs:
                term = weighted[j] if i == 0 else basis[i] * weighted[j]
                out.append(sums[place[(i, j)]] + term)
            seen = obs[date, here, :]
            for i in range(count):
                out.append(sums[len(pairs) + i] + seen * weighted[i])
            return tuple(out)

        zero = jnp.zeros((SUB, cols), jnp.float32)
        sums = lax.fori_loop(
            0, dates, date_step, (zero,) * (len(pairs) + count), unroll=2
        )
        share = land[here, :].astype(jnp.float32) * (1.0 / dates)
        rise_scale, fall_scale = 0.25 * rise_rate, 0.25 * fall_rate
        scale = [None, 0.5, -0.5, -rise_scale, rise_scale, fall_scale, -fall_scale]
        shared = [share] + [share * item for item in scale[1:]]
        block = {}
        for i, j in pairs:
            factor = shared[j] if i == 0 else shared[j] * scale[i]
            block[(i, j)] = sums[place[(i, j)]] * factor
        for p in range(count):
            total = shared[p] * sums[len(pairs) + p]
            for q, value in ((0, base), (1, peak), (2, slope)):
                total = total - block[(min(p, q), max(p, q))] * value
            resid[0, p, here, :] = total
        for p in range(count):
            block[(p, p)] = block[(p, p)] + (DAMPING + 4.0 * spatial[p] + 2.0 * temporal[p])
        for k in range(count):
            turn = 1.0 / block[(k, k)]
            edge = {i: block[(min(i, k), max(i, k))] for i in range(count) if i != k}
            lean = {i: edge[i] * turn for i in edge}
            for i, j in pairs:
                if i != k and j != k:
                    block[(i, j)] = block[(i, j)] - edge[i] * lean[j]
            for i in edge:
                block[(min(i, k), max(i, k))] = lean[i]
            block[(k, k)] = -turn
        for pair in pairs:
            inverse[place[pair], here, :] = -block[pair]

    zero = jnp.zeros((SUB, cols), jnp.float32)

    def make_stage(stage):
        def body(position, carry):
            odd_sum, even_sum = carry
            start = chunk_rows(position)
            first, last = position == 0, position == chunks - 1
            if stage == 0:
                for copy in input_loads(position):
                    copy.wait()

                def each(b, c):
                    normal(pl.multiple_of(start + b * SUB, SUB))
                    return c

                lax.fori_loop(0, BLOCKS, each, 0)
            before = stage
            wait_sides(before, position)
            wait_edges(before, first, last)
            for b in range(BLOCKS):
                at = pl.multiple_of(start + b * SUB, SUB)
                rows_here = pl.ds(at, SUB)
                held, pushed = [], []
                for p in range(count):
                    here, push = around(before, p, at)
                    if stage == 0:
                        push = (resid[0, p, rows_here, :] + push) - (
                            4.0 * spatial[p] + 2.0 * temporal[p]
                        ) * here
                    resid[stage, p, rows_here, :] = push
                    held.append(here)
                    pushed.append(push)
                if stage > 0:
                    odd_sum = odd_sum + dot(held, pushed)
                if stage < ITERS:
                    turned = precondition(at, pushed)
                    for p in range(count):
                        field[stage + 1, 0, p, pl.ds(at + SUB, SUB), :] = turned[p]
                    even_sum = even_sum + dot(turned, pushed)
            if stage < ITERS:
                start_sends(stage + 1, position)
                close_edges(stage + 1, first, last)
            return odd_sum, even_sum

        return body

    sums = []
    for stage in range(ITERS + 1):
        odd_sum, even_sum = lax.fori_loop(0, chunks, make_stage(stage), (zero, zero))
        if stage > 0:
            sums.append(odd_sum)
        if stage < ITERS:
            sums.append(even_sum)

    for at, value in enumerate(sums):
        moments[0, at : at + 1, :] = jnp.sum(value, axis=0, keepdims=True)

    def plane_copy(other):
        spot = lax.rem(row * n_col + col + other, n_row * n_col)
        return pltpu.make_async_remote_copy(
            src_ref=moments.at[0],
            dst_ref=plane_slots.at[other - 1],
            send_sem=plane_send.at[other - 1],
            recv_sem=plane_recv.at[other - 1],
            device_id=(year, spot // n_col, lax.rem(spot, n_col)),
            device_id_type=MESH,
        )

    def line_copy(other):
        return pltpu.make_async_remote_copy(
            src_ref=moments.at[1],
            dst_ref=year_slots.at[other - 1],
            send_sem=line_send.at[other - 1],
            recv_sem=line_recv.at[other - 1],
            device_id=(lax.rem(year + other, n_year), row, col),
            device_id_type=MESH,
        )

    for other in range(1, n_row * n_col):
        plane_copy(other).start()
    total = moments[0]
    for other in range(1, n_row * n_col):
        plane_copy(other).wait_recv()
        total = total + plane_slots[other - 1]
    moments[1] = total
    for other in range(1, n_year):
        line_copy(other).start()
    for other in range(1, n_year):
        line_copy(other).wait_recv()
        total = total + year_slots[other - 1]
    total = jnp.broadcast_to(jnp.sum(total, axis=1, keepdims=True), total.shape)
    mu = [total[at : at + 1, :] for at in range(2 * ITERS)]
    drop = [mu[at] - mu[at + 1] for at in range(2 * ITERS - 1)]

    def form(coefs, table):
        total = None
        for i, left in enumerate(coefs):
            for j in range(i, len(coefs)):
                term = left * coefs[j] * table[i + j]
                term = term if i == j else 2.0 * term
                total = term if total is None else total + term
        return total

    one = jnp.ones_like(mu[0])
    search, direction = [one], [one]
    lengths = [jnp.zeros_like(one)] * ITERS
    inner = mu[0]
    for sweep in range(ITERS):
        alpha = inner / form(direction, drop)
        for j in range(sweep + 1):
            lengths[j] = lengths[j] + alpha * direction[j]
        if sweep + 1 < ITERS:
            grown = []
            for j in range(sweep + 2):
                change = None
                if j <= sweep:
                    change = direction[j]
                if j > 0:
                    change = -direction[j - 1] if change is None else change - direction[j - 1]
                base = search[j] if j <= sweep else None
                grown.append(-alpha * change if base is None else base - alpha * change)
            search = grown
            fresh = form(search, mu)
            ratio = fresh / inner
            inner = fresh
            direction = [
                search[j] + ratio * direction[j] if j <= sweep else search[j]
                for j in range(sweep + 2)
            ]

    steps = [jnp.broadcast_to(value, (SUB, cols)) for value in lengths]
    mixes = [1.0 - steps[0]]
    mixes += [steps[j - 1] - steps[j] for j in range(1, ITERS)]
    mixes += [steps[-1]]

    def finish(b, carry):
        at = pl.multiple_of(b * SUB, SUB)
        rows_here = pl.ds(at, SUB)
        padded = pl.ds(at + SUB, SUB)
        for p in range(count):
            total = field[0, 0, p, padded, :]
            for j in range(ITERS):
                total = total + steps[j] * field[j + 1, 0, p, padded, :]
            new_params[0, p, rows_here, :] = total
            total = mixes[0] * resid[0, p, rows_here, :]
            for j in range(1, ITERS + 1):
                total = total + mixes[j] * resid[j, p, rows_here, :]
            residual[0, p, rows_here, :] = total
        return carry

    lax.fori_loop(0, rows // SUB, finish, 0)

    for step in range(ROUNDS):
        def drain(position, carry, step=step):
            for side in range(4):
                @pl.when(sides[side][0])
                def _(side=side):
                    side_copy(step, position, side).wait_send()
            return carry

        lax.fori_loop(0, chunks, drain, 0)
        for at_last, present in ((False, has_first), (True, has_last)):
            @pl.when(present)
            def _(at_last=at_last, step=step):
                row_copy(step, at_last).wait_send()
    for other in range(1, n_row * n_col):
        plane_copy(other).wait_send()
    for other in range(1, n_year):
        line_copy(other).wait_send()


def per_device(sizes, observed, quality, land_mask, params, spatial_weight, temporal_weight):
    n_year, n_row, n_col = sizes
    _, dates, rows, cols = observed.shape
    count = params.shape[1]
    chunks = rows // (SUB * BLOCKS)
    f32 = jnp.float32
    vmem = pl.BlockSpec(memory_space=pltpu.VMEM)
    hbm = pl.BlockSpec(memory_space=pltpu.HBM)
    smem = pl.BlockSpec(memory_space=pltpu.SMEM)
    dma = pltpu.SemaphoreType.DMA
    return pl.pallas_call(
        functools.partial(kernel, sizes),
        out_shape=(
            jax.ShapeDtypeStruct(params.shape, f32),
            jax.ShapeDtypeStruct(params.shape, f32),
        ),
        in_specs=[hbm, hbm, vmem, hbm, smem, smem],
        out_specs=(vmem, vmem),
        scratch_shapes=[
            pltpu.VMEM((dates, rows, cols), f32),
            pltpu.VMEM((dates, rows, cols), jnp.int32),
            pltpu.VMEM((ROUNDS, 5, count, rows + 2 * SUB, cols), f32),
            pltpu.VMEM((count * (count + 1) // 2, rows, cols), f32),
            pltpu.VMEM((ROUNDS, count, rows, cols), f32),
            pltpu.VMEM((2, 2 * ITERS, cols), f32),
            pltpu.VMEM((max(n_row * n_col - 1, 1), 2 * ITERS, cols), f32),
            pltpu.VMEM((max(n_year - 1, 1), 2 * ITERS, cols), f32),
            dma((1 + 2 * chunks,)),
            dma((ROUNDS, 4, chunks)),
            dma((ROUNDS, 4, chunks)),
            dma((ROUNDS, 2)),
            dma((ROUNDS, 2)),
            dma((max(n_row * n_col - 1, 1),)),
            dma((max(n_row * n_col - 1, 1),)),
            dma((max(n_year - 1, 1),)),
            dma((max(n_year - 1, 1),)),
        ],
        compiler_params=pltpu.CompilerParams(
            collective_id=0, has_side_effects=True, vmem_limit_bytes=48 * 1024 * 1024
        ),
        name="gauss_newton",
    )(observed, quality, land_mask, params, spatial_weight, temporal_weight)


def solution(mesh):
    sizes = tuple(mesh.shape[axis] for axis in ("year", "row", "col"))
    grid = P("year", None, "row", "col")
    return jax.shard_map(
        functools.partial(per_device, sizes),
        mesh=mesh,
        in_specs=(grid, grid, P("row", "col"), grid, P(), P()),
        out_specs=(grid, grid),
        check_vma=False,
    )
```

time: 384 us -> 52.8 us (0.14)
  blocking collectives: 173 us -> 0 us
  starting transfers between devices: 74.9 us -> 0 us
  Pallas kernels: 0 us -> 44.7 us
  other arithmetic: 40.5 us -> 0 us
  waiting for transfers between devices: 38.4 us -> 0 us
  between operations: 25.2 us -> 0.65 us
  local copies, waits for them, and re-layouts: 29.6 us -> 7.14 us
    psum x4 -> x0, blocking collectives: 173 us -> none  [paired_totals(): lax.psum((jnp.sum(residual * search), jnp.sum(image * search)), ('year',...]
    ppermute x30 -> x0, starting transfers between devices: 74.9 us -> none  [the longest x15 55.3 us: with_halo(): lax.ppermute(tail, axis, [(i, (i + 1) % count) for i in range(ends)])]
    pallas_call x0 -> x1, Pallas kernels: none -> 44.7 us  [per_device(): pl.pallas_call(functools.partial(kernel, sizes), out_shape=(jax.ShapeDtyp...]
    ppermute x30 -> x0, waiting for transfers between devices: 38.4 us -> none  [the longest x15 25.7 us: with_halo(): lax.ppermute(head, axis, [((i + 1) % count, i) for i in range(ends)])]
    reduce_sum x5 -> x0, other arithmetic: 17.7 us -> none  [the longest x4 9.9 us: paired_totals(): jnp.sum(image * search)]
    slice x18 -> x0, local copies, waits for them, and re-layouts: 15.8 us -> none  [the longest x11 10.3 us: with_halo(): lax.slice_in_dim(cells, cells.shape[dim] - width, cells.shape[dim], axis=...]
    ppermute x20 -> x0, local copies, waits for them, and re-layouts: 8.71 us -> none  [the longest x10 6.01 us: with_halo(): lax.ppermute(head, axis, [((i + 1) % count, i) for i in range(ends)])]
    unnamed x24 -> x0, other arithmetic: 8.22 us -> none
  transfers between devices with their start and end apart: 30 -> 0, of which waited for: 18 -> 0; matrix products, arithmetic and copies ran while one was open for 7% -> 0% of each run, Pallas kernels for 0% -> 0%
where the time goes in v1:
time: 52.8 us; the launch traced here: 52.5 us
  Pallas kernels  44.7 us (85%)
  local copies, waits for them, and re-layouts  7.14 us (14%)
  between operations  0.65 us (1%)
    pallas_call x1, Pallas kernels, per_device(): pl.pallas_call(functools.partial(kernel, sizes), out_shape=(jax.ShapeDtyp...  44.7 us
    unnamed x14, local copies, waits for them, and re-layouts  7.14 us

profile of v1, /device:TPU:0, one launch (start us, length us, event | category | flops | bytes accessed | tf_op | source)
XLA Modules:
  0.0 52.5 jit_solution(11530889781351592743)
XLA Ops:
  0.6 0.0 copy-start
  0.6 1.4 %copy-done = f32[1,46,64,128]{3,2,1,0:T(8,128)S(1)} copy-done((f32[1,46,64,128]{3,2,1,0:T(8,128)S(1)}, f32[1,46,64,128]{3,2,1,0:T(8,128)}, u32[]{:S(2)}) %copy-start) | copy-done | bytes 1507352
  2.0 0.0 copy-start.1
  2.0 1.4 %copy-done.1 = s32[1,46,64,128]{3,2,1,0:T(8,128)S(1)} copy-done((s32[1,46,64,128]{3,2,1,0:T(8,128)S(1)}, s32[1,46,64,128]{3,2,1,0:T(8,128)}, u32[]{:S(2)}) %copy-start.1) | copy-done | bytes 1507352
  3.4 0.0 copy-start.2
  3.4 0.9 %copy-done.2 = f32[1,7,64,128]{3,2,1,0:T(8,128)S(1)} copy-done((f32[1,7,64,128]{3,2,1,0:T(8,128)S(1)}, f32[1,7,64,128]{3,2,1,0:T(8,128)}, u32[]{:S(2)}) %copy-start.2) | copy-done | bytes 229400
  4.3 0.0 copy-start.3
  4.3 0.8 %copy-done.3 = s32[64,128]{1,0:T(8,128)S(1)} copy-done((s32[64,128]{1,0:T(8,128)S(1)}, s32[64,128]{1,0:T(8,128)}, u32[]{:S(2)}) %copy-start.3) | copy-done | bytes 32792
  5.1 0.0 copy-start.4
  5.1 0.7 %copy-done.4 = f32[7]{0:T(128)S(1)} copy-done((f32[7]{0:T(128)S(1)}, f32[7]{0:T(128)}, u32[]{:S(2)}) %copy-start.4) | copy-done | bytes 52
  5.8 0.0 copy-start.5
  5.8 0.7 %copy-done.5 = f32[7]{0:T(128)S(1)} copy-done((f32[7]{0:T(128)S(1)}, f32[7]{0:T(128)}, u32[]{:S(2)}) %copy-start.5) | copy-done | bytes 52
  6.4 44.7 %gauss_newton.1 = (f32[1,7,64,128]{3,2,1,0:T(8,128)S(1)}, f32[1,7,64,128]{3,2,1,0:T(8,128)S(1)}) custom-call(f32[1,46,64,128]{3,2,1,0:T(8,128)S(1)} %copy-done, s32[1,46,64,128]{3,2,1,0:T(8,128)S(1)} %copy-done.1, s32[64,128]{1,0:T(8,128)S(1)} %copy-done.3, f32[1,7,64,128]{3,2,1,0:T(8,128)S(1)} %copy-done.2, f32[7]{0:T(128)S(1)} %copy-done.4, f32[7]{0:T(128)S(1)} %copy-done.5), custom_call_target="tpu_custom_call" | custom-call | tf_op jit(solution)/shard_map/gauss_newton/pallas_call | solution.py:481
  51.1 0.7 %copy.10 = f32[1,7,64,128]{3,2,1,0:T(8,128)} copy(f32[1,7,64,128]{3,2,1,0:T(8,128)S(1)} %get-tuple-element.4) | data formatting | bytes 458752
  51.8 0.7 %copy.11 = f32[1,7,64,128]{3,2,1,0:T(8,128)} copy(f32[1,7,64,128]{3,2,1,0:T(8,128)S(1)} %get-tuple-element.5) | data formatting | bytes 458752
Async XLA Ops:
  0.6 1.4 %copy-start = (f32[1,46,64,128]{3,2,1,0:T(8,128)S(1)}, f32[1,46,64,128]{3,2,1,0:T(8,128)}, u32[]{:S(2)}) copy-start(f32[1,46,64,128]{3,2,1,0:T(8,128)} %observed.1) | copy-start | bytes 4521988
  2.0 1.4 %copy-start.1 = (s32[1,46,64,128]{3,2,1,0:T(8,128)S(1)}, s32[1,46,64,128]{3,2,1,0:T(8,128)}, u32[]{:S(2)}) copy-start(s32[1,46,64,128]{3,2,1,0:T(8,128)} %quality.1) | copy-start | bytes 4521988
  3.4 0.9 %copy-start.2 = (f32[1,7,64,128]{3,2,1,0:T(8,128)S(1)}, f32[1,7,64,128]{3,2,1,0:T(8,128)}, u32[]{:S(2)}) copy-start(f32[1,7,64,128]{3,2,1,0:T(8,128)} %params.1) | copy-start | bytes 688132
  4.3 0.8 %copy-start.3 = (s32[64,128]{1,0:T(8,128)S(1)}, s32[64,128]{1,0:T(8,128)}, u32[]{:S(2)}) copy-start(s32[64,128]{1,0:T(8,128)} %land.1) | copy-start | bytes 98308
  5.1 0.7 %copy-start.4 = (f32[7]{0:T(128)S(1)}, f32[7]{0:T(128)}, u32[]{:S(2)}) copy-start(f32[7]{0:T(128)} %spatial.1) | copy-start | bytes 88
  5.8 0.7 %copy-start.5 = (f32[7]{0:T(128)S(1)}, f32[7]{0:T(128)}, u32[]{:S(2)}) copy-start(f32[7]{0:T(128)} %temporal.1) | copy-start | bytes 88

commit v2 on v1

--- a/solution.py
+++ b/solution.py
@@ -506,7 +506,7 @@
             dma((max(n_year - 1, 1),)),
         ],
         compiler_params=pltpu.CompilerParams(
-            collective_id=0, has_side_effects=True, vmem_limit_bytes=48 * 1024 * 1024
+            collective_id=0, has_side_effects=True, vmem_limit_bytes=67043328
         ),
         name="gauss_newton",
     )(observed, quality, land_mask, params, spatial_weight, temporal_weight)

time: 52.8 us -> 49.5 us (0.938)
  local copies, waits for them, and re-layouts: 7.14 us -> 3.28 us
  Pallas kernels: 44.7 us -> 45.3 us
    unnamed x14 -> x2, local copies, waits for them, and re-layouts: 7.14 us -> 3.28 us
    pallas_call x1, Pallas kernels: 44.7 us -> 45.3 us  [per_device(): pl.pallas_call(functools.partial(kernel, sizes), out_shape=(jax.ShapeDtyp...]
where the time goes in v2:
time: 49.5 us; the launch traced here: 49.2 us
  Pallas kernels  45.3 us (92%)
  local copies, waits for them, and re-layouts  3.28 us (7%)
  between operations  0.64 us (1%)
    pallas_call x1, Pallas kernels, per_device(): pl.pallas_call(functools.partial(kernel, sizes), out_shape=(jax.ShapeDtyp...  45.3 us
    unnamed x2, local copies, waits for them, and re-layouts  3.28 us

profile of v2, /device:TPU:0, one launch (start us, length us, event | category | flops | bytes accessed | tf_op | source)
XLA Modules:
  0.0 49.2 jit_solution(9151825110595054995)
XLA Ops:
  0.6 45.3 %gauss_newton.1 = (f32[1,7,64,128]{3,2,1,0:T(8,128)}, f32[1,7,64,128]{3,2,1,0:T(8,128)}) custom-call(f32[1,46,64,128]{3,2,1,0:T(8,128)} %observed.1, s32[1,46,64,128]{3,2,1,0:T(8,128)} %quality.1, s32[64,128]{1,0:T(8,128)} %land.1, f32[1,7,64,128]{3,2,1,0:T(8,128)} %params.1, f32[7]{0:T(128)} %spatial.1, f32[7]{0:T(128)} %temporal.1), custom_call_target="tpu_custom_call" | custom-call | tf_op jit(solution)/shard_map/gauss_newton/pallas_call | solution.py:481
  46.0 1.6 %copy.10 = f32[1,7,64,128]{3,2,1,0:T(8,128)} copy(f32[1,7,64,128]{3,2,1,0:T(8,128)} %get-tuple-element.4) | data formatting | bytes 458752
  47.6 1.6 %copy.11 = f32[1,7,64,128]{3,2,1,0:T(8,128)} copy(f32[1,7,64,128]{3,2,1,0:T(8,128)} %get-tuple-element.5) | data formatting | bytes 458752

commit v3 on v2

--- a/solution.py
+++ b/solution.py
@@ -35,17 +35,14 @@
     inverse,
     resid,
     moments,
-    plane_slots,
-    year_slots,
+    slots,
     load_sem,
     send_sem,
     recv_sem,
     row_send,
     row_recv,
-    plane_send,
-    plane_recv,
-    line_send,
-    line_recv,
+    sum_send,
+    sum_recv,
 ):
     n_year, n_row, n_col = sizes
     dates, rows, cols = obs.shape
@@ -87,17 +84,39 @@
         for copy in input_loads(position):
             copy.start()
 
+    total_devices = n_year * n_row * n_col
+    near = (n_year - 1) + (n_row - 1) <= ITERS
+
+    def peer(other):
+        spot = lax.rem((year * n_row + row) * n_col + col + other, total_devices)
+        return (spot // (n_row * n_col), lax.rem(spot // n_col, n_row), lax.rem(spot, n_col))
+
     barrier = pltpu.get_barrier_semaphore()
-    for other in range(1, n_row * n_col):
-        spot = lax.rem(row * n_col + col + other, n_row * n_col)
-        pl.semaphore_signal(
-            barrier, inc=1, device_id=(year, spot // n_col, lax.rem(spot, n_col)), device_id_type=MESH
-        )
-    for other in range(1, n_year):
-        pl.semaphore_signal(
-            barrier, inc=1, device_id=(lax.rem(year + other, n_year), row, col), device_id_type=MESH
-        )
-    pl.semaphore_wait(barrier, n_row * n_col + n_year - 2)
+    if near:
+        for other in range(1, n_col):
+            pl.semaphore_signal(
+                barrier,
+                inc=1,
+                device_id=(year, row, lax.rem(col + other, n_col)),
+                device_id_type=MESH,
+            )
+        expected = n_col - 1
+        for present, target in (
+            (has_prev, (year - 1, row, col)),
+            (has_next, (year + 1, row, col)),
+            (has_up, (year, row - 1, col)),
+            (has_down, (year, row + 1, col)),
+        ):
+            @pl.when(present)
+            def _(target=target):
+                pl.semaphore_signal(barrier, inc=1, device_id=target, device_id_type=MESH)
+
+            expected = expected + present.astype(jnp.int32)
+        pl.semaphore_wait(barrier, expected)
+    else:
+        for other in range(1, total_devices):
+            pl.semaphore_signal(barrier, inc=1, device_id=peer(other), device_id_type=MESH)
+        pl.semaphore_wait(barrier, total_devices - 1)
 
     sides = (
         (has_next, (year + 1, row, col), 1, has_prev),
@@ -267,7 +286,7 @@
 
         zero = jnp.zeros((SUB, cols), jnp.float32)
         sums = lax.fori_loop(
-            0, dates, date_step, (zero,) * (len(pairs) + count), unroll=2
+            0, dates, date_step, (zero,) * (len(pairs) + count), unroll=dates
         )
         share = land[here, :].astype(jnp.float32) * (1.0 / dates)
         rise_scale, fall_scale = 0.25 * rise_rate, 0.25 * fall_rate
@@ -352,41 +371,27 @@
             sums.append(even_sum)
 
     for at, value in enumerate(sums):
-        moments[0, at : at + 1, :] = jnp.sum(value, axis=0, keepdims=True)
-
-    def plane_copy(other):
-        spot = lax.rem(row * n_col + col + other, n_row * n_col)
+        moments[at : at + 1, :] = jnp.sum(value, axis=0, keepdims=True)
+
+    def sum_copy(other):
         return pltpu.make_async_remote_copy(
-            src_ref=moments.at[0],
-            dst_ref=plane_slots.at[other - 1],
-            send_sem=plane_send.at[other - 1],
-            recv_sem=plane_recv.at[other - 1],
-            device_id=(year, spot // n_col, lax.rem(spot, n_col)),
+            src_ref=moments,
+            dst_ref=slots.at[other - 1],
+            send_sem=sum_send.at[other - 1],
+            recv_sem=sum_recv.at[other - 1],
+            device_id=peer(other),
             device_id_type=MESH,
         )
 
-    def line_copy(other):
-        return pltpu.make_async_remote_copy(
-            src_ref=moments.at[1],
-            dst_ref=year_slots.at[other - 1],
-            send_sem=line_send.at[other - 1],
-            recv_sem=line_recv.at[other - 1],
-            device_id=(lax.rem(year + other, n_year), row, col),
-            device_id_type=MESH,
-        )
-
-    for other in range(1, n_row * n_col):
-        plane_copy(other).start()
-    total = moments[0]
-    for other in range(1, n_row * n_col):
-        plane_copy(other).wait_recv()
-        total = total + plane_slots[other - 1]
-    moments[1] = total
-    for other in range(1, n_year):
-        line_copy(other).start()
-    for other in range(1, n_year):
-        line_copy(other).wait_recv()
-        total = total + year_slots[other - 1]
+    for other in range(1, total_devices):
+        sum_copy(other).start()
+    parts = [moments[...]]
+    for other in range(1, total_devices):
+        sum_copy(other).wait_recv()
+        parts.append(slots[other - 1])
+    while len(parts) > 1:
+        parts = [sum(parts[i : i + 2][1:], parts[i]) for i in range(0, len(parts), 2)]
+    total = parts[0]
     total = jnp.broadcast_to(jnp.sum(total, axis=1, keepdims=True), total.shape)
     mu = [total[at : at + 1, :] for at in range(2 * ITERS)]
     drop = [mu[at] - mu[at + 1] for at in range(2 * ITERS - 1)]
@@ -462,10 +467,8 @@
             @pl.when(present)
             def _(at_last=at_last, step=step):
                 row_copy(step, at_last).wait_send()
-    for other in range(1, n_row * n_col):
-        plane_copy(other).wait_send()
-    for other in range(1, n_year):
-        line_copy(other).wait_send()
+    for other in range(1, total_devices):
+        sum_copy(other).wait_send()
 
 
 def per_device(sizes, observed, quality, land_mask, params, spatial_weight, temporal_weight):
@@ -473,6 +476,7 @@
     _, dates, rows, cols = observed.shape
     count = params.shape[1]
     chunks = rows // (SUB * BLOCKS)
+    others = n_year * n_row * n_col - 1
     f32 = jnp.float32
     vmem = pl.BlockSpec(memory_space=pltpu.VMEM)
     hbm = pl.BlockSpec(memory_space=pltpu.HBM)
@@ -492,18 +496,15 @@
             pltpu.VMEM((ROUNDS, 5, count, rows + 2 * SUB, cols), f32),
             pltpu.VMEM((count * (count + 1) // 2, rows, cols), f32),
             pltpu.VMEM((ROUNDS, count, rows, cols), f32),
-            pltpu.VMEM((2, 2 * ITERS, cols), f32),
-            pltpu.VMEM((max(n_row * n_col - 1, 1), 2 * ITERS, cols), f32),
-            pltpu.VMEM((max(n_year - 1, 1), 2 * ITERS, cols), f32),
+            pltpu.VMEM((2 * ITERS, cols), f32),
+            pltpu.VMEM((max(others, 1), 2 * ITERS, cols), f32),
             dma((1 + 2 * chunks,)),
             dma((ROUNDS, 4, chunks)),
             dma((ROUNDS, 4, chunks)),
             dma((ROUNDS, 2)),
             dma((ROUNDS, 2)),
-            dma((max(n_row * n_col - 1, 1),)),
-            dma((max(n_row * n_col - 1, 1),)),
-            dma((max(n_year - 1, 1),)),
-            dma((max(n_year - 1, 1),)),
+            dma((max(others, 1),)),
+            dma((max(others, 1),)),
         ],
         compiler_params=pltpu.CompilerParams(
             collective_id=0, has_side_effects=True, vmem_limit_bytes=67043328

time: 49.5 us -> 44.9 us (0.907)
  Pallas kernels: 45.3 us -> 40.7 us
    pallas_call x1, Pallas kernels: 45.3 us -> 40.7 us  [per_device(): pl.pallas_call(functools.partial(kernel, sizes), out_shape=(jax.ShapeDtyp...]
where the time goes in v3:
time: 44.9 us; the launch traced here: 44.6 us
  Pallas kernels  40.7 us (91%)
  local copies, waits for them, and re-layouts  3.28 us (7%)
  between operations  0.64 us (1%)
    pallas_call x1, Pallas kernels, per_device(): pl.pallas_call(functools.partial(kernel, sizes), out_shape=(jax.ShapeDtyp...  40.7 us
    unnamed x2, local copies, waits for them, and re-layouts  3.28 us

profile of v3, /device:TPU:0, one launch (start us, length us, event | category | flops | bytes accessed | tf_op | source)
XLA Modules:
  0.0 44.6 jit_solution(1937611257487608807)
XLA Ops:
  0.6 40.7 %gauss_newton.1 = (f32[1,7,64,128]{3,2,1,0:T(8,128)}, f32[1,7,64,128]{3,2,1,0:T(8,128)}) custom-call(f32[1,46,64,128]{3,2,1,0:T(8,128)} %observed.1, s32[1,46,64,128]{3,2,1,0:T(8,128)} %quality.1, s32[64,128]{1,0:T(8,128)} %land.1, f32[1,7,64,128]{3,2,1,0:T(8,128)} %params.1, f32[7]{0:T(128)} %spatial.1, f32[7]{0:T(128)} %temporal.1), custom_call_target="tpu_custom_call" | custom-call | tf_op jit(solution)/shard_map/gauss_newton/pallas_call | solution.py:485
  41.3 1.6 %copy.10 = f32[1,7,64,128]{3,2,1,0:T(8,128)} copy(f32[1,7,64,128]{3,2,1,0:T(8,128)} %get-tuple-element.4) | data formatting | bytes 458752
  43.0 1.6 %copy.11 = f32[1,7,64,128]{3,2,1,0:T(8,128)} copy(f32[1,7,64,128]{3,2,1,0:T(8,128)} %get-tuple-element.5) | data formatting | bytes 458752

commit v4 on v3

--- a/solution.py
+++ b/solution.py
@@ -385,6 +385,19 @@
 
     for other in range(1, total_devices):
         sum_copy(other).start()
+    for step in range(ROUNDS):
+        def drain(position, carry, step=step):
+            for side in range(4):
+                @pl.when(sides[side][0])
+                def _(side=side):
+                    side_copy(step, position, side).wait_send()
+            return carry
+
+        lax.fori_loop(0, chunks, drain, 0)
+        for at_last, present in ((False, has_first), (True, has_last)):
+            @pl.when(present)
+            def _(at_last=at_last, step=step):
+                row_copy(step, at_last).wait_send()
     parts = [moments[...]]
     for other in range(1, total_devices):
         sum_copy(other).wait_recv()
@@ -454,19 +467,6 @@
 
     lax.fori_loop(0, rows // SUB, finish, 0)
 
-    for step in range(ROUNDS):
-        def drain(position, carry, step=step):
-            for side in range(4):
-                @pl.when(sides[side][0])
-                def _(side=side):
-                    side_copy(step, position, side).wait_send()
-            return carry
-
-        lax.fori_loop(0, chunks, drain, 0)
-        for at_last, present in ((False, has_first), (True, has_last)):
-            @pl.when(present)
-            def _(at_last=at_last, step=step):
-                row_copy(step, at_last).wait_send()
     for other in range(1, total_devices):
         sum_copy(other).wait_send()
 

time: 44.9 us -> 44.5 us (level)
  no operation moved by 1% of the time
where the time goes in v4:
time: 44.5 us; the launch traced here: 44.3 us
  Pallas kernels  40.4 us (91%)
  local copies, waits for them, and re-layouts  3.28 us (7%)
  between operations  0.64 us (1%)
    pallas_call x1, Pallas kernels, per_device(): pl.pallas_call(functools.partial(kernel, sizes), out_shape=(jax.ShapeDtyp...  40.4 us
    unnamed x2, local copies, waits for them, and re-layouts  3.28 us

profile of v4, /device:TPU:0, one launch (start us, length us, event | category | flops | bytes accessed | tf_op | source)
XLA Modules:
  0.0 44.3 jit_solution(15578810598347944270)
XLA Ops:
  0.6 40.4 %gauss_newton.1 = (f32[1,7,64,128]{3,2,1,0:T(8,128)}, f32[1,7,64,128]{3,2,1,0:T(8,128)}) custom-call(f32[1,46,64,128]{3,2,1,0:T(8,128)} %observed.1, s32[1,46,64,128]{3,2,1,0:T(8,128)} %quality.1, s32[64,128]{1,0:T(8,128)} %land.1, f32[1,7,64,128]{3,2,1,0:T(8,128)} %params.1, f32[7]{0:T(128)} %spatial.1, f32[7]{0:T(128)} %temporal.1), custom_call_target="tpu_custom_call" | custom-call | tf_op jit(solution)/shard_map/gauss_newton/pallas_call | solution.py:485
  41.0 1.6 %copy.10 = f32[1,7,64,128]{3,2,1,0:T(8,128)} copy(f32[1,7,64,128]{3,2,1,0:T(8,128)} %get-tuple-element.4) | data formatting | bytes 458752
  42.7 1.6 %copy.11 = f32[1,7,64,128]{3,2,1,0:T(8,128)} copy(f32[1,7,64,128]{3,2,1,0:T(8,128)} %get-tuple-element.5) | data formatting | bytes 458752
